TPU v7x, 32 devices: a whole 2x2x4 slice. The times are simulated.
32 devices in a mesh: groups: 2 (over y), hist: 4 (over z), head: 2 (over x), rep: 2 (over core).
Axes of the slice: x: 2, y: 2, z: 4, core: 2. Of those that a mesh axis runs over, the one named last changes fastest.
Arguments:
- item_feats: bfloat16 [4096, 4096], P(('groups', 'hist', 'rep')), parts along dimension 0, may hold values from -6 to 6
- adapter: bfloat16 [4096, 512], P('hist', 'head'), may hold values from -0.09375 to 0.09375
- hist_emb: bfloat16 [8192, 512], P(('groups', 'hist')), parts along dimension 0, may hold values from -6 to 6
- key_weight: bfloat16 [512, 512], P(None, 'head'), may hold values from -0.25 to 0.25
- value_weight: bfloat16 [512, 512], P(None, 'head'), may hold values from -0.25 to 0.25
- routes: int32 [4096, 1], P(('groups', 'hist', 'rep')), parts along dimension 0, may hold values from 0 to 3; in each aligned block of 256 rows (0 to 255, 256 to 511, ...) at most 128 rows name the same one
- cand_index: int32 [1024], P(('groups', 'hist', 'rep')), parts along dimension 0, may hold values from 0 to 255
- item_user: int32 [4096], P(('groups', 'hist', 'rep')), parts along dimension 0, may hold values from 0 to 255
- hist_user: int32 [8192], P(('groups', 'hist')), parts along dimension 0, may hold values from 0 to 255
Outputs:
- scored: bfloat16 [1024, 512], P(('groups', 'hist', 'rep'), 'head'), parts along dimension 0
There are 2 independent parts, one for each index of `groups`. A program takes and returns all parts, laid end to end along the dimension named above; an argument that names none is the same for every part. Nothing has to cross between parts.
Inputs may be any that keep to these rules, and one draw needn't show every extreme that they name: `routes`: in the rows of one device no owner is named more than 128 times; some owner is named exactly 128 times.
All inputs are finite; a program needn't handle non-finite values.
Results may differ from a plain program's by a relative error of at most 0.0081.
Values may be sent and summed in bfloat16 or wider, within the bound.
A program may use at most 64 MiB of HBM per device.

v0:
```python
import math
import jax
import jax.numpy as jnp
from jax import lax
from jax.sharding import PartitionSpec as P

HS = 64


def attend(query_block, user_block, key_rows, value_rows, key_users):
    row_count = query_block.shape[0]
    col_count = query_block.shape[1]
    heads_here = col_count // HS
    att_scale = float(HS) ** (-0.5)
    query_three = query_block.reshape(row_count, heads_here, HS)
    key_three = key_rows.reshape(-1, heads_here, HS)
    value_three = value_rows.reshape(-1, heads_here, HS)
    scores = (
        jnp.einsum("rhd,khd->hrk", query_three, key_three, preferred_element_type=jnp.float32)
        * att_scale
    )
    matching = user_block[:, None] == key_users[None, :]
    weights = jnp.where(matching[None], jax.nn.silu(scores), 0.0).astype(jnp.bfloat16)
    mixture = jnp.einsum("hrk,khd->rhd", weights, value_three, preferred_element_type=jnp.float32)
    counted = jnp.sum(matching.astype(jnp.float32), axis=1)
    inverse = 1.0 / jnp.maximum(counted, 1.0)
    return mixture.reshape(row_count, col_count) * inverse[:, None]


def dense_partial(queries, users, key_rows, value_rows, key_users):
    total_rows = queries.shape[0]
    col_count = queries.shape[1]
    block_size = math.gcd(total_rows, 512)
    blocked_queries = queries.reshape(total_rows // block_size, block_size, col_count)
    blocked_users = users.reshape(total_rows // block_size, block_size)

    def one_block(operands):
        return attend(operands[0], operands[1], key_rows, value_rows, key_users)

    return lax.map(one_block, (blocked_queries, blocked_users)).reshape(total_rows, col_count)


def body(
    item_feats,
    adapter,
    hist_emb,
    key_weight,
    value_weight,
    routes,
    cand_index,
    item_user,
    hist_user,
):
    owners = lax.axis_size("hist")
    item_count = item_feats.shape[0]
    col_count = adapter.shape[1]
    embedded = jnp.dot(
        item_feats,
        lax.all_gather(adapter, "hist", axis=0, tiled=True),
        preferred_element_type=jnp.float32,
    ).astype(jnp.bfloat16)
    capacity = 2 * item_count // owners
    owner_of = routes[:, 0]
    owner_hot = (owner_of[:, None] == jnp.arange(owners, dtype=jnp.int32)[None, :]).astype(
        jnp.int32
    )
    earlier = jnp.cumsum(owner_hot, axis=0) - owner_hot
    slot_of = jnp.sum(earlier * owner_hot, axis=1)
    position = owner_of * capacity + slot_of
    placing = (jnp.arange(owners * capacity, dtype=jnp.int32)[:, None] == position[None, :]).astype(
        jnp.bfloat16
    )
    outgoing = jnp.dot(placing, embedded, preferred_element_type=jnp.float32).astype(jnp.bfloat16)
    outgoing = outgoing.reshape(owners, capacity, col_count)
    shifted_user = (item_user + 1).astype(jnp.bfloat16)
    outgoing_user = (
        jnp.dot(placing, shifted_user, preferred_element_type=jnp.float32) - 1.0
    ).astype(jnp.bfloat16)
    outgoing_user = outgoing_user.reshape(owners, capacity)
    incoming, incoming_user = (
        lax.all_to_all(outgoing, "hist", split_axis=0, concat_axis=0, tiled=True),
        lax.all_to_all(outgoing_user, "hist", split_axis=0, concat_axis=0, tiled=True),
    )
    routed, routed_user = (
        lax.all_gather(incoming, "rep", axis=0, tiled=True),
        lax.all_gather(incoming_user, "rep", axis=0, tiled=True),
    )
    routed = routed.reshape(-1, col_count)
    routed_user = routed_user.reshape(-1)
    key_local = jnp.dot(hist_emb, key_weight, preferred_element_type=jnp.float32).astype(
        jnp.bfloat16
    )
    value_local = jnp.dot(hist_emb, value_weight, preferred_element_type=jnp.float32).astype(
        jnp.bfloat16
    )
    key_rows = jnp.concatenate([key_local, routed], axis=0)
    value_rows = jnp.concatenate([value_local, routed], axis=0)
    key_users = jnp.concatenate([hist_user.astype(jnp.bfloat16), routed_user], axis=0)
    own_queries = embedded[cand_index]
    own_users = item_user[cand_index].astype(jnp.bfloat16)
    gathered, gathered_users = (
        lax.all_gather(own_queries, "hist", axis=0, tiled=True),
        lax.all_gather(own_users, "hist", axis=0, tiled=True),
    )
    partial_value = dense_partial(gathered, gathered_users, key_rows, value_rows, key_users)
    attended = lax.psum_scatter(partial_value, "hist", scatter_dimension=0, tiled=True)
    gating = jax.nn.silu(own_queries.astype(jnp.float32))
    return (gating * attended).astype(jnp.bfloat16)


def solution(mesh):
    placed = (
        P(("groups", "hist", "rep"), None),
        P("hist", "head"),
        P(("groups", "hist"), None),
        P(None, "head"),
        P(None, "head"),
        P(("groups", "hist", "rep"), None),
        P(("groups", "hist", "rep")),
        P(("groups", "hist", "rep")),
        P(("groups", "hist")),
    )
    return jax.shard_map(
        body,
        mesh=mesh,
        in_specs=placed,
        out_specs=P(("groups", "hist", "rep"), "head"),
        check_vma=False,
    )
```

profile of v0, /device:TPU:0, one launch (start us, length us, event | category | flops | bytes accessed | tf_op | source)
XLA Modules:
  0.0 119.3 jit_solution(5111718014451120370)
XLA Ops:
  6.5 0.0 copy-start
  6.5 0.0 copy-start.1
  6.5 0.0 copy-start.2
  6.5 0.0 copy-start.5
  6.5 0.0 copy-start.6
  6.5 0.0 all-gather.4.cloned.1.call-start
  6.6 0.7 all-gather.4.cloned.1.call-update
  7.3 0.8 add_convert_fusion.1
  8.1 0.7 compare_convert_fusion
  8.7 1.2 %reduce-window.6 = s32[4,2,128]{2,1,0:T(2,128)S(1)} reduce-window(s32[4,2,128]{2,1,0:T(2,128)S(1)} %compare_convert_fusion, s32[]{:T(128)} %constant.17.clone.1), window={size=1x1x128 pad=0_0x0_0x127_0}, to_apply=%region_0.0 | reduce-window | flops 130048 | bytes 8196 | tf_op jit(solution)/shard_map/reduce-window
  10.0 0.1 slice.12
  10.0 0.1 copy.20
  10.2 0.1 copy.21
  10.3 0.1 add_bitcast_fusion
  10.3 0.7 fusion.14
  11.0 0.7 multiply_add_fusion
  11.7 0.2 fusion.4
  11.9 0.6 copy.23
  12.5 6.3 %all-to-all-start.1 = ((bf16[4,1,128]{2,1,0:T(2,128)(2,1)}), bf16[4,1,128]{2,1,0:T(2,128)(2,1)S(1)}, u32[]{:S(2)}, u32[]{:S(2)}) async-start(bf16[4,1,128]{2,1,0:T(2,128)(2,1)} %copy.23), calls=%async_computation.1 | async-start | bytes 4096 | tf_op jit(solution)/shard_map/all_to_all | solution.py:82
  18.9 0.7 compare_select_fusion
  19.5 0.0 copy-start.7
  19.5 2.7 %convolution_convert_fusion = bf16[1024,256]{0,1:T(8,128)(2,1)} fusion(bf16[1024,512]{1,0:T(8,128)(2,1)} %param.11, bf16[512,256]{1,0:T(8,128)(2,1)} %param.12), kind=kOutput, calls=%fused_computation.5 | convolution fusion | flops 268697600 | bytes 1835008 | tf_op jit(solution)/shard_map/dot_general | solution.py:90
  22.2 0.0 copy-done.2
  22.2 0.0 copy-done.5
  22.2 1.3 %convolution_convert_fusion.1 = bf16[1024,256]{0,1:T(8,128)(2,1)} fusion(bf16[1024,512]{1,0:T(8,128)(2,1)S(1)} %copy-done.2, bf16[512,256]{1,0:T(8,128)(2,1)S(1)} %copy-done.5), kind=kOutput, calls=%fused_computation.6 | convolution fusion | flops 268697600 | bytes 1835008 | tf_op jit(solution)/shard_map/dot_general | solution.py:93
  23.5 0.0 copy-done.6
  23.5 0.0 copy-done.1
  23.6 0.8 gather_fusion.1
  24.4 0.0 copy-done.7
  24.4 0.6 dynamic-slice.2
  25.5 0.2 dynamic-update-slice
  25.7 12.6 %all-reduce = bf16[256]{0:T(256)(128)(2,1)S(1)} all-reduce(bf16[256]{0:T(256)(128)(2,1)S(1)} %dynamic-update-slice), channel_id=1, replica_groups=mesh['groups'=2,'hist'=4,'head'=2,'rep'=2] {'hist'}, use_global_device_ids=true, to_apply=%add | all-reduce | flops 256 | bytes 1024
  38.4 0.0 all-to-all-done.1
  38.4 1.8 %all-gather = bf16[8,1,128]{2,1,0:T(2,128)(2,1)S(1)} all-gather(bf16[4,1,128]{2,1,0:T(2,128)(2,1)S(1)} %all-to-all-done.1), channel_id=2, replica_groups=mesh['groups'=2,'hist'=4,'head'=2,'rep'=2] {'rep'}, dimensions={0}, use_global_device_ids=true | all-gather | bytes 3072 | tf_op jit(solution)/shard_map/all_gather | solution.py:86
  40.2 0.4 convert_reduce_fusion
  40.6 17.1 %all-gather.4.cloned.1.call-done = bf16[4096,256]{1,0:T(8,128)(2,1)} async-done(((bf16[1024,256]{1,0:T(8,128)(2,1)}), bf16[4096,256]{1,0:T(8,128)(2,1)}) %all-gather.4.cloned.1.call-update) | async-done | bytes 2097168 | tf_op jit(solution)/shard_map/all_gather | solution.py:59
  57.7 0.0 copy-done
  57.7 2.3 %convolution_convert_fusion.3 = bf16[256,256]{1,0:T(8,128)(2,1)S(1)} fusion(bf16[256,4096]{1,0:T(8,128)(2,1)S(1)} %copy-done, bf16[4096,256]{1,0:T(8,128)(2,1)} %all-gather.4.cloned.1.call-done), kind=kOutput, calls=%fused_computation.10 | convolution fusion | flops 536936448 | bytes 4325376 | tf_op jit(solution)/shard_map/dot_general | solution.py:57
  60.0 0.9 convolution_convert_fusion.2
  60.9 3.4 %all-to-all-start = ((bf16[4,128,256]{2,1,0:T(8,128)(2,1)}), bf16[4,128,256]{2,1,0:T(8,128)(2,1)S(1)}, u32[]{:S(2)}, u32[]{:S(2)}) async-start(bf16[4,128,256]{2,1,0:T(8,128)(2,1)} %bitcast.5), calls=%async_computation | async-start | bytes 524288 | tf_op jit(solution)/shard_map/all_to_all | solution.py:81
  64.3 0.0 reduce-scatter.2.cloned.1.call-start
  64.4 1.1 broadcast_compare_fusion
  65.5 0.7 gather_fusion
  66.2 0.0 copy-start.3
  66.2 14.3 %all-gather.1 = bf16[256,256]{1,0:T(8,128)(2,1)S(1)} all-gather(bf16[64,256]{1,0:T(8,128)(2,1)S(1)} %gather_fusion), channel_id=3, replica_groups=mesh['groups'=2,'hist'=4,'head'=2,'rep'=2] {'hist'}, dimensions={0}, use_global_device_ids=true | all-gather | bytes 163840 | tf_op jit(solution)/shard_map/all_gather | solution.py:102
  80.5 0.8 copy.24
  81.3 0.0 copy-done.3
  81.3 0.0 all-to-all-done
  81.3 2.2 %all_gather.16 = bf16[8,128,256]{2,1,0:T(8,128)(2,1)S(1)} all-gather(bf16[4,128,256]{2,1,0:T(8,128)(2,1)S(1)} %all-to-all-done), channel_id=1, replica_groups=mesh['groups'=2,'hist'=4,'head'=2,'rep'=2] {'rep'}, dimensions={0}, use_global_device_ids=true | all-gather | bytes 786432 | tf_op jit(solution)/shard_map/all_gather | solution.py:85
  83.5 0.3 copy.22
  83.8 0.2 concatenate.18
  84.0 0.0 copy-start.4
  84.0 5.2 %fusion = f32[4,64,256]{2,1,0:T(8,128)S(1)} fusion(bf16[256,4,64]{0,2,1:T(8,128)(2,1)} %bitcast.47, pred[256,2048]{1,0:T(8,128)(4,1)} %broadcast_compare_fusion, bf16[1024,4,64]{0,2,1:T(8,128)(2,1)S(1)} %concatenate.18, bf16[1024,4,64]{0,2,1:T(8,128)(2,1)} %bitcast.45, bf16[1024,4,64]{0,2,1:T(8,128)(2,1)} %bitcast.44), kind=kOutput, calls=%fused_computation.4 | convolution fusion | flops 555745280 | bytes 2490368 | tf_op jit(solution)/shard_map/while/body/eval_jaxpr/hrk,khd->rhd/dot_general | solution.py:24
  89.3 0.1 copy.25
  89.4 0.8 broadcast_multiply_fusion
  90.2 0.0 reduce-scatter.2.cloned.1.call-update
  90.2 20.8 %reduce-scatter.2.cloned.1.call-done = f32[64,256]{1,0:T(8,128)} async-done(((f32[256,256]{1,0:T(8,128)}), f32[64,256]{1,0:T(8,128)}) %reduce-scatter.2.cloned.1.call-update) | async-done | bytes 65552 | tf_op jit(solution)/shard_map/reduce_scatter | solution.py:106
  111.0 0.0 copy-done.4
  111.0 1.5 %fusion.11 = bf16[64,256]{1,0:T(8,128)(2,1)} fusion(f32[64,256]{1,0:T(8,128)} %reduce-scatter.2.cloned.1.call-done, bf16[64,256]{1,0:T(8,128)(2,1)S(1)} %copy-done.4), kind=kLoop, calls=%fused_computation.25 | loop fusion | flops 114688 | bytes 131072 | tf_op jit(solution)/shard_map/convert_element_type | solution.py:108
  (11 shorter events, 0.1 us)
Async XLA Ops:
  6.5 51.1 %copy-start = (bf16[256,4096]{1,0:T(8,128)(2,1)S(1)}, bf16[256,4096]{1,0:T(8,128)(2,1)}, u32[]{:S(2)}) copy-start(bf16[256,4096]{1,0:T(8,128)(2,1)} %param.9) | copy-start | bytes 6291460
  6.5 17.0 %copy-start.1 = (s32[256]{0:T(256)S(1)}, s32[256]{0:T(256)}, u32[]{:S(2)}) copy-start(s32[256]{0:T(256)} %param.16) | copy-start | bytes 3076
  6.5 15.7 %copy-start.2 = (bf16[1024,512]{1,0:T(8,128)(2,1)S(1)}, bf16[1024,512]{1,0:T(8,128)(2,1)}, u32[]{:S(2)}) copy-start(bf16[1024,512]{1,0:T(8,128)(2,1)} %param.11) | copy-start | bytes 3145732
  6.5 15.7 %copy-start.5 = (bf16[512,256]{1,0:T(8,128)(2,1)S(1)}, bf16[512,256]{1,0:T(8,128)(2,1)}, u32[]{:S(2)}) copy-start(bf16[512,256]{1,0:T(8,128)(2,1)} %param.13) | copy-start | bytes 786436
  6.5 17.0 %copy-start.6 = (s32[1024]{0:T(1024)S(1)}, s32[1024]{0:T(1024)}, u32[]{:S(2)}) copy-start(s32[1024]{0:T(1024)} %param.17) | copy-start | bytes 12292
  6.5 51.1 %all-gather.4.cloned.1.call-start = ((), (), s32[]{:S(2)}) async-start(), calls=%async_computation.3 | async-start | bytes 2621440 | tf_op jit(solution)/shard_map/all_gather | solution.py:59
  12.5 25.8 %all-to-all-start.1 = ((bf16[4,1,128]{2,1,0:T(2,128)(2,1)}), bf16[4,1,128]{2,1,0:T(2,128)(2,1)S(1)}, u32[]{:S(2)}, u32[]{:S(2)}) async-start(bf16[4,1,128]{2,1,0:T(2,128)(2,1)} %copy.23), calls=%async_computation.1 | async-start | bytes 4096 | tf_op jit(solution)/shard_map/all_to_all | solution.py:82
  19.5 4.8 %copy-start.7 = (u32[32]{0:T(128)S(1)}, u32[32]{0:T(128)}, u32[]{:S(2)}) copy-start(u32[32]{0:T(128)} %constant.42) | copy-start | bytes 388
  60.9 20.4 %all-to-all-start = ((bf16[4,128,256]{2,1,0:T(8,128)(2,1)}), bf16[4,128,256]{2,1,0:T(8,128)(2,1)S(1)}, u32[]{:S(2)}, u32[]{:S(2)}) async-start(bf16[4,128,256]{2,1,0:T(8,128)(2,1)} %bitcast.5), calls=%async_computation | async-start | bytes 524288 | tf_op jit(solution)/shard_map/all_to_all | solution.py:81
  64.3 46.7 %reduce-scatter.2.cloned.1.call-start = ((), (), s32[]{:S(2)}) async-start(), calls=%async_computation.4 | async-start | bytes 327680 | tf_op jit(solution)/shard_map/reduce_scatter | solution.py:106
  66.2 15.1 %copy-start.3 = (bf16[64,256]{1,0:T(8,128)(2,1)}, bf16[64,256]{1,0:T(8,128)(2,1)S(1)}, u32[]{:S(2)}) copy-start(bf16[64,256]{1,0:T(8,128)(2,1)S(1)} %gather_fusion) | copy-start | bytes 98308
  84.0 27.0 %copy-start.4 = (bf16[64,256]{1,0:T(8,128)(2,1)S(1)}, bf16[64,256]{1,0:T(8,128)(2,1)}, u32[]{:S(2)}) copy-start(bf16[64,256]{1,0:T(8,128)(2,1)} %copy-done.3) | copy-start | bytes 98308
Sparse Core Ops, SparseCore 0:
  8.9 48.7 all-gather.3
  90.3 20.6 reduce-scatter.1
where the time goes:
time: 120 us; the launch traced here: 119 us
  waiting for transfers between devices  38.6 us (32%)
  blocking collectives  30.9 us (26%)
  between operations  14.1 us (12%)
  matrix products  12.7 us (11%)
  starting transfers between devices  9.83 us (8%)
  other arithmetic  8.64 us (7%)
  local copies, waits for them, and re-layouts  4.62 us (4%)
    reduce_scatter x1, waiting for transfers between devices, body(): lax.psum_scatter(partial_value, 'hist', scatter_dimension=0, tiled=True)  20.8 us
    all_gather x1, waiting for transfers between devices, body(): lax.all_gather(adapter, 'hist', axis=0, tiled=True)  17.1 us
    all_gather x1, blocking collectives, body(): lax.all_gather(own_queries, 'hist', axis=0, tiled=True)  14.3 us
    unnamed x1, blocking collectives  12.6 us
    all_to_all x1, starting transfers between devices, body(): lax.all_to_all(outgoing_user, 'hist', split_axis=0, concat_axis=0, tiled=...  6.35 us
    dot_general x1, matrix products, attend(): jnp.einsum('hrk,khd->rhd', weights, value_three, preferred_element_type=j...  5.22 us
    all_to_all x1, starting transfers between devices, body(): lax.all_to_all(outgoing, 'hist', split_axis=0, concat_axis=0, tiled=True)  3.4 us
    dot_general x1, matrix products, body(): jnp.dot(hist_emb, key_weight, preferred_element_type=jnp.float32)  2.69 us
  transfers between devices with their start and end apart: 4, of which 2 were waited for; matrix products, arithmetic and copies ran while one was open for 12% of the time, Pallas kernels for 0%

commit v1 on v0

--- a/solution.py
+++ b/solution.py
@@ -56,7 +56,9 @@
     col_count = adapter.shape[1]
     embedded = jnp.dot(
         item_feats,
-        lax.all_gather(adapter, "hist", axis=0, tiled=True),
+        jnp.concatenate(
+            lax.all_to_all(jnp.stack([adapter] * lax.axis_size("hist")), "hist", 0, 0), axis=0
+        ),
         preferred_element_type=jnp.float32,
     ).astype(jnp.bfloat16)
     capacity = 2 * item_count // owners

time: 120 us -> 147 us (1.23)
  blocking collectives: 30.9 us -> 66.8 us
  waiting for transfers between devices: 38.6 us -> 23.3 us
  starting transfers between devices: 9.83 us -> 15.2 us
  local copies, waits for them, and re-layouts: 4.62 us -> 6.55 us
    unnamed x1, blocking collectives: 12.6 us -> 36.5 us
    all_gather x1 -> x0, waiting for transfers between devices: 17.1 us -> none  [body(): lax.all_gather(adapter, 'hist', axis=0, tiled=True)]
    all_to_all x0 -> x1, blocking collectives: none -> 11.7 us  [body(): lax.all_to_all(outgoing_user, 'hist', split_axis=0, concat_axis=0, tiled=...]
    all_to_all x1, starting transfers between devices: 3.4 us -> 10.6 us  [body(): lax.all_to_all(outgoing, 'hist', split_axis=0, concat_axis=0, tiled=True)]
    all_to_all x1, waiting for transfers between devices: 0.01 us -> 2.66 us  [body(): lax.all_to_all(jnp.stack([adapter] * lax.axis_size('hist')), 'hist', 0, 0)]
    another operation x2 -> x3, local copies, waits for them, and re-layouts: 0.1 us -> 2.57 us  [the longest x1 2.47 us: body(): jnp.stack([adapter] * lax.axis_size('hist'))]
    all_to_all x1, starting transfers between devices: 6.35 us -> 4.58 us  [body(): lax.all_to_all(jnp.stack([adapter] * lax.axis_size('hist')), 'hist', 0, 0)]
  transfers between devices with their start and end apart: 4 -> 3, of which waited for: 2 -> 2; matrix products, arithmetic and copies ran while one was open for 12% -> 6% of each run, Pallas kernels for 0% -> 0%
where the time goes in v1:
time: 147 us; the launch traced here: 146 us
  blocking collectives  66.8 us (45%)
  waiting for transfers between devices  23.3 us (16%)
  starting transfers between devices  15.2 us (10%)
  between operations  14.2 us (10%)
  matrix products  12.2 us (8%)
  other arithmetic  8.05 us (5%)
  local copies, waits for them, and re-layouts  6.55 us (4%)
    unnamed x1, blocking collectives  36.5 us
    reduce_scatter x1, waiting for transfers between devices, body(): lax.psum_scatter(partial_value, 'hist', scatter_dimension=0, tiled=True)  20.6 us
    all_gather x1, blocking collectives, body(): lax.all_gather(own_queries, 'hist', axis=0, tiled=True)  14.5 us
    all_to_all x1, blocking collectives, body(): lax.all_to_all(outgoing_user, 'hist', split_axis=0, concat_axis=0, tiled=...  11.7 us
    all_to_all x1, starting transfers between devices, body(): lax.all_to_all(outgoing, 'hist', split_axis=0, concat_axis=0, tiled=True)  10.6 us
    dot_general x1, matrix products, attend(): jnp.einsum('hrk,khd->rhd', weights, value_three, preferred_element_type=j...  5.23 us
    all_to_all x1, starting transfers between devices, body(): lax.all_to_all(jnp.stack([adapter] * lax.axis_size('hist')), 'hist', 0, 0)  4.58 us
  transfers between devices with their start and end apart: 3, of which 2 were waited for; matrix products, arithmetic and copies ran while one was open for 6% of the time, Pallas kernels for 0%

profile of v1, /device:TPU:0, one launch (start us, length us, event | category | flops | bytes accessed | tf_op | source)
XLA Modules:
  0.0 146.4 jit_solution(7994627517315313999)
XLA Ops:
  6.5 0.0 copy-start
  6.5 0.8 add_convert_fusion.1
  7.4 0.7 compare_convert_fusion
  8.1 1.2 reduce-window.6
  9.3 0.1 slice.12
  9.3 0.1 copy.20
  9.5 0.1 copy.21
  9.6 0.1 add_bitcast_fusion
  9.7 0.7 fusion.14
  10.4 0.7 multiply_add_fusion
  11.0 0.2 fusion.4
  11.3 11.7 %all_to_all.22 = bf16[4,1,128]{2,1,0:T(2,128)(2,1)S(1)} all-to-all(bf16[4,1,128]{2,1,0:T(2,128)(2,1)S(1)} %copy.23), channel_id=1, replica_groups=mesh['groups'=2,'hist'=4,'head'=2,'rep'=2] {'hist'}, dimensions={0} | all-to-all | bytes 2048 | tf_op jit(solution)/shard_map/all_to_all | solution.py:84
  23.0 2.5 %stack.2 = bf16[4,1024,256]{2,1,0:T(8,128)(2,1)} broadcast(bf16[1024,256]{1,0:T(8,128)(2,1)} %param.10), dimensions={1,2} | broadcast | bytes 2621440 | tf_op jit(solution)/shard_map/stack | solution.py:60
  25.5 0.0 copy-start.6
  25.5 0.0 copy-start.7
  25.5 0.0 copy-start.1
  25.5 0.0 copy-start.8
  25.5 0.0 copy-start.2
  25.5 0.0 copy-start.5
  25.5 4.6 %all-to-all-start = ((bf16[4,1024,256]{2,1,0:T(8,128)(2,1)}), bf16[4,1024,256]{2,1,0:T(8,128)(2,1)}, u32[]{:S(2)}, u32[]{:S(2)}) async-start(bf16[4,1024,256]{2,1,0:T(8,128)(2,1)} %stack.2), calls=%async_computation | async-start | bytes 4194304 | tf_op jit(solution)/shard_map/all_to_all | solution.py:60
  30.1 0.0 copy-done.6
  30.1 0.0 copy-done.7
  30.1 0.0 copy-done.1
  30.2 0.8 gather_fusion.1
  31.0 0.0 copy-done.8
  31.0 0.6 dynamic-slice.2
  32.2 0.2 dynamic-update-slice
  32.5 36.5 %all-reduce = bf16[256]{0:T(256)(128)(2,1)S(1)} all-reduce(bf16[256]{0:T(256)(128)(2,1)S(1)} %dynamic-update-slice), channel_id=1, replica_groups=mesh['groups'=2,'hist'=4,'head'=2,'rep'=2] {'hist'}, use_global_device_ids=true, to_apply=%add | all-reduce | flops 256 | bytes 1024
  69.0 0.0 copy-done.2
  69.0 0.0 copy-done.5
  69.0 1.3 convolution_convert_fusion.1
  70.3 2.3 %convolution_convert_fusion = bf16[1024,256]{0,1:T(8,128)(2,1)} fusion(bf16[1024,512]{1,0:T(8,128)(2,1)S(1)} %copy-done.2, bf16[512,256]{1,0:T(8,128)(2,1)} %param.12), kind=kOutput, calls=%fused_computation.5 | convolution fusion | flops 268697600 | bytes 1835008 | tf_op jit(solution)/shard_map/dot_general | solution.py:92
  72.5 1.8 %all-gather = bf16[8,1,128]{2,1,0:T(2,128)(2,1)S(1)} all-gather(bf16[4,1,128]{2,1,0:T(2,128)(2,1)S(1)} %all_to_all.22), channel_id=2, replica_groups=mesh['groups'=2,'hist'=4,'head'=2,'rep'=2] {'rep'}, dimensions={0}, use_global_device_ids=true | all-gather | bytes 3072 | tf_op jit(solution)/shard_map/all_gather | solution.py:88
  74.4 0.4 convert_reduce_fusion
  74.7 2.7 %all-to-all-done = bf16[4,1024,256]{2,1,0:T(8,128)(2,1)} async-done(((bf16[4,1024,256]{2,1,0:T(8,128)(2,1)}), bf16[4,1024,256]{2,1,0:T(8,128)(2,1)}, u32[]{:S(2)}, u32[]{:S(2)}) %all-to-all-start) | async-done | bytes 2097184 | tf_op jit(solution)/shard_map/all_to_all | solution.py:60
  77.4 0.0 copy-done
  77.4 2.3 %convolution_convert_fusion.3 = bf16[256,256]{1,0:T(8,128)(2,1)S(1)} fusion(bf16[256,4096]{1,0:T(8,128)(2,1)S(1)} %copy-done, bf16[4096,256]{1,0:T(8,128)(2,1)} %bitcast), kind=kOutput, calls=%fused_computation.10 | convolution fusion | flops 536936448 | bytes 4325376 | tf_op jit(solution)/shard_map/dot_general | solution.py:57
  79.7 0.9 convolution_convert_fusion.2
  80.7 10.6 %all-to-all-start.1 = ((bf16[4,128,256]{2,1,0:T(8,128)(2,1)}), bf16[4,128,256]{2,1,0:T(8,128)(2,1)S(1)}, u32[]{:S(2)}, u32[]{:S(2)}) async-start(bf16[4,128,256]{2,1,0:T(8,128)(2,1)} %bitcast.6), calls=%async_computation.1 | async-start | bytes 524288 | tf_op jit(solution)/shard_map/all_to_all | solution.py:83
  91.3 0.0 reduce-scatter.2.cloned.1.call-start
  91.3 1.1 broadcast_compare_fusion
  92.4 0.7 gather_fusion
  93.1 0.0 copy-start.3
  93.1 14.5 %all-gather.1 = bf16[256,256]{1,0:T(8,128)(2,1)S(1)} all-gather(bf16[64,256]{1,0:T(8,128)(2,1)S(1)} %gather_fusion), channel_id=3, replica_groups=mesh['groups'=2,'hist'=4,'head'=2,'rep'=2] {'hist'}, dimensions={0}, use_global_device_ids=true | all-gather | bytes 163840 | tf_op jit(solution)/shard_map/all_gather | solution.py:104
  107.7 0.8 copy.24
  108.4 0.0 copy-done.3
  108.4 0.0 all-to-all-done.1
  108.4 2.2 %all_gather.12 = bf16[8,128,256]{2,1,0:T(8,128)(2,1)S(1)} all-gather(bf16[4,128,256]{2,1,0:T(8,128)(2,1)S(1)} %all-to-all-done.1), channel_id=1, replica_groups=mesh['groups'=2,'hist'=4,'head'=2,'rep'=2] {'rep'}, dimensions={0}, use_global_device_ids=true | all-gather | bytes 786432 | tf_op jit(solution)/shard_map/all_gather | solution.py:87
  110.6 0.3 copy.22
  110.9 0.2 concatenate.18
  111.2 0.0 copy-start.4
  111.2 5.2 %fusion = f32[4,64,256]{2,1,0:T(8,128)S(1)} fusion(bf16[256,4,64]{0,2,1:T(8,128)(2,1)} %bitcast.48, pred[256,2048]{1,0:T(8,128)(4,1)} %broadcast_compare_fusion, bf16[1024,4,64]{0,2,1:T(8,128)(2,1)S(1)} %concatenate.18, bf16[1024,4,64]{0,2,1:T(8,128)(2,1)} %bitcast.45, bf16[1024,4,64]{0,2,1:T(8,128)(2,1)} %bitcast.46), kind=kOutput, calls=%fused_computation.4 | convolution fusion | flops 555745280 | bytes 2490368 | tf_op jit(solution)/shard_map/while/body/eval_jaxpr/hrk,khd->rhd/dot_general | solution.py:24
  116.4 0.1 copy.25
  116.6 0.8 broadcast_multiply_fusion
  117.3 0.0 reduce-scatter.2.cloned.1.call-update
  117.4 20.6 %reduce-scatter.2.cloned.1.call-done = f32[64,256]{1,0:T(8,128)} async-done(((f32[256,256]{1,0:T(8,128)}), f32[64,256]{1,0:T(8,128)}) %reduce-scatter.2.cloned.1.call-update) | async-done | bytes 65552 | tf_op jit(solution)/shard_map/reduce_scatter | solution.py:108
  138.0 0.0 copy-done.4
  138.0 1.5 %fusion.11 = bf16[64,256]{1,0:T(8,128)(2,1)} fusion(f32[64,256]{1,0:T(8,128)} %reduce-scatter.2.cloned.1.call-done, bf16[64,256]{1,0:T(8,128)(2,1)S(1)} %copy-done.4), kind=kLoop, calls=%fused_computation.25 | loop fusion | flops 114688 | bytes 131072 | tf_op jit(solution)/shard_map/convert_element_type | solution.py:110
  (13 shorter events, 0.1 us)
Async XLA Ops:
  6.5 70.9 %copy-start = (bf16[256,4096]{1,0:T(8,128)(2,1)S(1)}, bf16[256,4096]{1,0:T(8,128)(2,1)}, u32[]{:S(2)}) copy-start(bf16[256,4096]{1,0:T(8,128)(2,1)} %param.9) | copy-start | bytes 6291460
  25.5 4.6 %copy-start.6 = (s32[1024]{0:T(1024)S(1)}, s32[1024]{0:T(1024)}, u32[]{:S(2)}) copy-start(s32[1024]{0:T(1024)} %param.17) | copy-start | bytes 12292
  25.5 4.7 %copy-start.7 = (s32[64]{0:T(128)S(1)}, s32[64]{0:T(128)}, u32[]{:S(2)}) copy-start(s32[64]{0:T(128)} %param.15) | copy-start | bytes 772
  25.5 4.7 %copy-start.1 = (s32[256]{0:T(256)S(1)}, s32[256]{0:T(256)}, u32[]{:S(2)}) copy-start(s32[256]{0:T(256)} %param.16) | copy-start | bytes 3076
  25.5 5.5 %copy-start.8 = (u32[32]{0:T(128)S(1)}, u32[32]{0:T(128)}, u32[]{:S(2)}) copy-start(u32[32]{0:T(128)} %constant.42) | copy-start | bytes 388
  25.5 43.5 %copy-start.2 = (bf16[1024,512]{1,0:T(8,128)(2,1)S(1)}, bf16[1024,512]{1,0:T(8,128)(2,1)}, u32[]{:S(2)}) copy-start(bf16[1024,512]{1,0:T(8,128)(2,1)} %param.11) | copy-start | bytes 3145732
  25.5 43.5 %copy-start.5 = (bf16[512,256]{1,0:T(8,128)(2,1)S(1)}, bf16[512,256]{1,0:T(8,128)(2,1)}, u32[]{:S(2)}) copy-start(bf16[512,256]{1,0:T(8,128)(2,1)} %param.13) | copy-start | bytes 786436
  25.5 51.9 %all-to-all-start = ((bf16[4,1024,256]{2,1,0:T(8,128)(2,1)}), bf16[4,1024,256]{2,1,0:T(8,128)(2,1)}, u32[]{:S(2)}, u32[]{:S(2)}) async-start(bf16[4,1024,256]{2,1,0:T(8,128)(2,1)} %stack.2), calls=%async_computation | async-start | bytes 4194304 | tf_op jit(solution)/shard_map/all_to_all | solution.py:60
  80.7 27.8 %all-to-all-start.1 = ((bf16[4,128,256]{2,1,0:T(8,128)(2,1)}), bf16[4,128,256]{2,1,0:T(8,128)(2,1)S(1)}, u32[]{:S(2)}, u32[]{:S(2)}) async-start(bf16[4,128,256]{2,1,0:T(8,128)(2,1)} %bitcast.6), calls=%async_computation.1 | async-start | bytes 524288 | tf_op jit(solution)/shard_map/all_to_all | solution.py:83
  91.3 46.7 %reduce-scatter.2.cloned.1.call-start = ((), (), s32[]{:S(2)}) async-start(), calls=%async_computation.4 | async-start | bytes 327680 | tf_op jit(solution)/shard_map/reduce_scatter | solution.py:108
  93.1 15.3 %copy-start.3 = (bf16[64,256]{1,0:T(8,128)(2,1)}, bf16[64,256]{1,0:T(8,128)(2,1)S(1)}, u32[]{:S(2)}) copy-start(bf16[64,256]{1,0:T(8,128)(2,1)S(1)} %gather_fusion) | copy-start | bytes 98308
  111.2 26.8 %copy-start.4 = (bf16[64,256]{1,0:T(8,128)(2,1)S(1)}, bf16[64,256]{1,0:T(8,128)(2,1)}, u32[]{:S(2)}) copy-start(bf16[64,256]{1,0:T(8,128)(2,1)} %copy-done.3) | copy-start | bytes 98308
Sparse Core Ops, SparseCore 0:
  117.5 20.4 reduce-scatter.1
